TPU v7x, 256 devices: a whole 4x4x8 slice. The times are simulated.
256 devices in a mesh: blk: 256 (over z, x, y, core).
Axes of the slice: x: 4, y: 4, z: 8, core: 2. Of those that a mesh axis runs over, the one named last changes fastest.
Arguments:
- blocks: float32 [4, 4096, 256, 128], P(None, 'blk'), may hold values from -6 to 6
- first: float32 [4096, 256], P('blk'), may hold values from -2.4 to 2.4
- second: float32 [65536, 256], P('blk'), may hold values from -2.4 to 2.4
- third: float32 [32768, 256], P('blk'), may hold values from -2.4 to 2.4
Outputs:
- first_final: float32 [4096, 256], P('blk')
- second_final: float32 [65536, 256], P('blk')
- third_final: float32 [32768, 256], P('blk')
All inputs are finite; a program needn't handle non-finite values.
Results may differ from a plain program's by a relative error of at most 0.0003.
Values sent between devices are 32-bit elements; how exact they have to be, the bound alone decides.
No kernel may reach another device: no remote copies, remote signals or barrier semaphores. Data moves between devices by JAX's collectives and lax.ppermute only.
A program may use at most 64 MiB of HBM per device.

v0:
```python
import jax
import jax.numpy as jnp
from jax import lax
from jax.experimental import pallas as pl
from jax.experimental.pallas import tpu as pltpu
from jax.sharding import PartitionSpec as P


momentum = 0.5
step_scale = 8.0
F32 = jnp.float32
BF16 = jnp.bfloat16


def sent(array, by):
    count = lax.axis_size("blk")
    return lax.ppermute(array, "blk", [(i, (i + by) % count) for i in range(count)])


def split(x):
    high = x.astype(BF16)
    return high, (x - high.astype(F32)).astype(BF16)


def dot(a, b):
    return jnp.dot(a, b, preferred_element_type=F32)


def dot3(a, b):
    return dot(a[0], b[0]) + dot(a[0], b[1]) + dot(a[1], b[0])


def gram(x):
    return dot3(split(x.T), split(x))


def vmem(n):
    return [pl.BlockSpec(memory_space=pltpu.VMEM)] * n


def like(*shape, dtype=F32):
    return jax.ShapeDtypeStruct(shape, dtype)


def kernel(body, out_shape, operands, in_specs=None, scratch_shapes=()):
    return pl.pallas_call(
        body,
        out_shape=tuple(out_shape),
        in_specs=in_specs or vmem(len(operands)),
        out_specs=tuple(vmem(len(out_shape))),
        scratch_shapes=scratch_shapes,
        compiler_params=pltpu.CompilerParams(vmem_limit_bytes=16 << 20),
        cost_estimate=pl.CostEstimate(flops=1 << 30, bytes_accessed=4 << 20, transcendentals=0),
    )(*operands)


def prepare(s, blocks):
    _, first_rows, second_rows, third_rows = blocks.shape
    pairs = first_rows // 2

    def body(target, natural_h, natural_l, turned_h, turned_l, buf, sem):
        def fetch(p):
            return pltpu.make_async_copy(target.at[s, pl.ds(2 * p, 2)], buf.at[p], sem.at[p])

        for p in range(pairs):
            fetch(p).start()
        for p in range(pairs):
            fetch(p).wait()
            for h in range(2):
                t = buf[p, h]
                span = slice((2 * p + h) * third_rows, (2 * p + h + 1) * third_rows)
                natural_h[:, span], natural_l[:, span] = split(t)
                turned_h[span, :], turned_l[span, :] = split(t.T)

    wide = first_rows * third_rows
    natural, turned = like(second_rows, wide, dtype=BF16), like(wide, second_rows, dtype=BF16)
    return kernel(
        body,
        (natural, natural, turned, turned),
        (pltpu.with_memory_space_constraint(blocks, pltpu.HBM),),
        in_specs=[pl.BlockSpec(memory_space=pltpu.HBM)],
        scratch_shapes=[
            pltpu.VMEM((pairs, 2, second_rows, third_rows), F32),
            pltpu.SemaphoreType.DMA((pairs,)),
        ],
    )


def second_side(first, third, older, natural_h, natural_l):
    first_rows, rank = first.shape
    third_rows = third.shape[0]
    second_rows, wide = natural_h.shape
    chunks = 4

    def body(a, c, *refs):
        if older is not None:
            o, refs = refs[0], refs[1:]
            c_now = c[...] - momentum * o[...]
        else:
            c_now = c[...]
        nat_h, nat_l, target_second, gram_first, gram_third = refs[:5]
        pair_h, pair_l = refs[-2:]
        if older is not None:
            refs[5][...] = c_now
        total = None
        for n in range(chunks):
            size = first_rows // chunks
            for i in range(n * size, (n + 1) * size):
                span = slice(i * third_rows, (i + 1) * third_rows)
                pair_h[span, :], pair_l[span, :] = split(a[i : i + 1, :] * c_now)
            span = slice(n * wide // chunks, (n + 1) * wide // chunks)
            part = dot3((nat_h[:, span], nat_l[:, span]), (pair_h[span, :], pair_l[span, :]))
            total = part if total is None else total + part
        target_second[...] = total
        gram_first[...] = gram(a[...])
        gram_third[...] = gram(c_now)

    olds = () if older is None else (older,)
    out = kernel(
        body,
        (like(second_rows, rank), like(rank, rank), like(rank, rank)) + ((like(third_rows, rank),) if olds else ()),
        (first, third, *olds, natural_h, natural_l),
        scratch_shapes=[pltpu.VMEM((wide, rank), BF16)] * 2,
    )
    return out if olds else (*out, third)


def update(s, strata, rates, turned, target_second, grams, factors, vel_first, old_second):
    first_rows, rank = factors[0].shape
    third_rows = factors[2].shape[0]
    ahead = 1.0 if s == 0 else 1.0 + momentum
    last = s + 1 == strata

    def body(turned_h, turned_l, t_second, gram_first, gram_third, *refs):
        a, b, c = (ref[...] for ref in refs[:3])
        rest = list(refs[3:])
        vel = momentum * rest.pop(0)[...] if s else None
        old = rest.pop(0)[...] if old_second is not None else None
        new_first, new_second, new_third = rest[:3]
        contracted = rest[-1]
        split_b = split(b)
        contracted[...] = dot3((turned_h[...], turned_l[...]), split_b)
        gram_second = dot3(split(b.T), split_b)

        g_second = dot3(split_b, split(gram_first[...] * gram_third[...])) - t_second[...]
        base = ahead * b if old is None else ahead * b - momentum * old
        new_second[...] = base - rates[1] * g_second

        g_third = jnp.zeros_like(c)
        rows = []
        for i in range(first_rows):
            part = contracted[i * third_rows : (i + 1) * third_rows, :]
            rows.append(jnp.sum(part * c, axis=0, keepdims=True))
            g_third = g_third + part * refs[0][i : i + 1, :]
        g_third = dot3(split(c), split(gram_first[...] * gram_second)) - g_third
        new_third[...] = ahead * c - rates[2] * g_third
        g_first = dot3(split(a), split(gram_second * gram_third[...])) - jnp.concatenate(rows, axis=0)
        step = rates[0] * g_first
        new_first[...] = a - step if vel is None else a + vel - step
        if not last:
            rest[3][...] = -step if vel is None else vel - step

    operands = (*turned, target_second, *grams, *factors)
    operands += (vel_first,) if s else ()
    operands += () if old_second is None else (old_second,)
    shapes = [pltpu.VMEM(factors[0].shape, F32) if last else like(*factors[0].shape)]
    shapes += [like(*x.shape) for x in factors[1:]] + ([] if last else [like(first_rows, rank)])
    return kernel(body, shapes, operands, scratch_shapes=[pltpu.VMEM((first_rows * third_rows, rank), F32)])


def shards(blocks, first, second, third):
    strata = 4
    first_rows = first.shape[0]
    second_rows = second.shape[0]
    third_rows = third.shape[0]
    rates = (
        step_scale / (second_rows * third_rows),
        step_scale / (first_rows * third_rows),
        step_scale / (first_rows * second_rows),
    )
    vel = None
    home_third = third
    old_second = old_third = None
    older = {}
    for s in range(strata):
        natural_h, natural_l, *turned = prepare(s, blocks)
        if s == 0:
            older["b1"] = sent(second, -1)
            older["c2"] = sent(third, -6)
        old_second, old_third = older.get(f"b{s}"), older.get(f"c{s}")
        target_second, *grams, third = second_side(first, third, old_third, natural_h, natural_l)
        first, second, third, *vel = update(
            s,
            strata,
            rates,
            turned,
            target_second,
            grams,
            (first, second, third),
            vel and vel[0],
            old_second,
        )
        if s == 0:
            older["b2"] = sent(second, -2)
            older["c3"] = sent(third, -9)
        if s == 1:
            back_second = sent(second, 1)
            back_third = sent(third, 3)
        if s + 1 < strata:
            third = sent(third, -3)
            second = sent(second, -1)
    third = sent(third, 3 * (strata - 1))
    second = sent(second, strata - 1)
    second = second - momentum * back_second
    third = third - momentum * (back_third - momentum * home_third)
    return (first, second, third)


def solution(mesh):
    placed = (P(None, "blk", None, None), P("blk", None), P("blk", None), P("blk", None))

    return jax.shard_map(
        shards,
        mesh=mesh,
        in_specs=placed,
        out_specs=(P("blk", None), P("blk", None), P("blk", None)),
        check_vma=False,
    )
```

profile of v0, /device:TPU:1, one launch (start us, length us, event | category | flops | bytes accessed | tf_op | source)
XLA Modules:
  0.0 84.4 jit_solution(12922545435478298763)
XLA Ops:
  0.7 2.4 %shard_map.70 = (bf16[256,2048]{1,0:T(8,128)(2,1)S(1)}, bf16[256,2048]{1,0:T(8,128)(2,1)S(1)}, bf16[2048,256]{1,0:T(8,128)(2,1)S(1)}, bf16[2048,256]{1,0:T(8,128)(2,1)S(1)}) custom-call(f32[4,16,256,128]{3,2,1,0:T(8,128)} %target.7), custom_call_target="tpu_custom_call" | custom-call | flops 1073741824 | bytes 4194304 | tf_op jit(solution)/shard_map/pallas_call | solution.py:46
  3.1 1.2 %shard_map.71 = (f32[256,256]{1,0:T(8,128)S(1)}, f32[256,256]{1,0:T(8,128)S(1)}, f32[256,256]{1,0:T(8,128)S(1)}) custom-call(f32[16,256]{1,0:T(8,128)S(1)} %copy-done.2, f32[128,256]{1,0:T(8,128)S(1)} %copy-done, bf16[256,2048]{1,0:T(8,128)(2,1)S(1)} %get-tuple-element.56.refs_0_, bf16[256,2048]{1,0:T(8,128)(2,1)S(1)} %get-tuple-element.57.refs_1_), custom_call_target="tpu_custom_call" | custom-call | flops 1073741824 | bytes 4194304 | tf_op jit(solution)/shard_map/pallas_call | solution.py:46
  4.3 1.4 %shard_map.72 = (f32[16,256]{1,0:T(8,128)S(1)}, f32[256,256]{1,0:T(8,128)S(1)}, f32[128,256]{1,0:T(8,128)S(1)}, f32[16,256]{1,0:T(8,128)S(1)}) custom-call(bf16[2048,256]{1,0:T(8,128)(2,1)S(1)} %get-tuple-element.54.turned_h, bf16[2048,256]{1,0:T(8,128)(2,1)S(1)} %get-tuple-element.55.turned_l, f32[256,256]{1,0:T(8,128)S(1)} %get-tuple-element.58.t_second, ...), custom_call_target="tpu_custom_call" | custom-call | flops 1073741824 | bytes 4194304 | tf_op jit(solution)/shard_map/pallas_call | solution.py:46
  5.7 3.3 %collective-permute-start.1 = (f32[256,256]{1,0:T(8,128)S(1)}, f32[256,256]{1,0:T(8,128)S(1)}, u32[]{:S(2)}, u32[]{:S(2)}) collective-permute-start(f32[256,256]{1,0:T(8,128)S(1)} %get-tuple-element.68), channel_id=1, source_target_pairs={{0,255},{1,0},{2,1},{3,2},{4,3},{5,4},{6,5},{7,6},{8,7},{9,8},{10,... | collective-permute-start | bytes 786440 | tf_op jit(solution)/shard_map/ppermute | solution.py:17
  9.0 8.2 %collective-permute-start.2 = (f32[256,256]{1,0:T(8,128)S(1)}, f32[256,256]{1,0:T(8,128)S(1)}, u32[]{:S(2)}, u32[]{:S(2)}) collective-permute-start(f32[256,256]{1,0:T(8,128)S(1)} %copy-done.1), channel_id=1, source_target_pairs={{0,255},{1,0},{2,1},{3,2},{4,3},{5,4},{6,5},{7,6},{8,7},{9,8},{10,... | collective-permute-start | bytes 786440 | tf_op jit(solution)/shard_map/ppermute | solution.py:17
  17.3 1.0 %collective-permute-start = (f32[128,256]{1,0:T(8,128)S(1)}, f32[128,256]{1,0:T(8,128)S(1)}, u32[]{:S(2)}, u32[]{:S(2)}) collective-permute-start(f32[128,256]{1,0:T(8,128)S(1)} %get-tuple-element.62), channel_id=1, source_target_pairs={{0,253},{1,254},{2,255},{3,0},{4,1},{5,2},{6,3},{7,4},{8,5},{9,6},... | collective-permute-start | bytes 393224 | tf_op jit(solution)/shard_map/ppermute | solution.py:17
  18.3 0.2 collective-permute-start.6
  18.5 2.4 %shard_map.69 = (bf16[256,2048]{1,0:T(8,128)(2,1)S(1)}, bf16[256,2048]{1,0:T(8,128)(2,1)S(1)}, bf16[2048,256]{1,0:T(8,128)(2,1)S(1)}, bf16[2048,256]{1,0:T(8,128)(2,1)S(1)}) custom-call(f32[4,16,256,128]{3,2,1,0:T(8,128)} %target.7), custom_call_target="tpu_custom_call" | custom-call | flops 1073741824 | bytes 4194304 | tf_op jit(solution)/shard_map/pallas_call | solution.py:46
  20.8 2.3 %collective-permute-done.c.refs_2_ = f32[128,256]{1,0:T(8,128)S(1)} collective-permute-done((f32[128,256]{1,0:T(8,128)S(1)}, f32[128,256]{1,0:T(8,128)S(1)}, u32[]{:S(2)}, u32[]{:S(2)}) %collective-permute-start) | collective-permute-done | bytes 131104 | tf_op jit(solution)/shard_map/ppermute | solution.py:17
  23.2 1.2 %shard_map.73 = (f32[256,256]{1,0:T(8,128)S(1)}, f32[256,256]{1,0:T(8,128)S(1)}, f32[256,256]{1,0:T(8,128)S(1)}) custom-call(f32[16,256]{1,0:T(8,128)S(1)} %get-tuple-element.61.a.refs_0_, f32[128,256]{1,0:T(8,128)S(1)} %collective-permute-done.c.refs_2_, bf16[256,2048]{1,0:T(8,128)(2,1)S(1)} %get-tuple-element.63.refs_0_, ...), custom_call_target="tpu_custom_call" | custom-call | flops 1073741824 | bytes 4194304 | tf_op jit(solution)/shard_map/pallas_call | solution.py:46
  24.4 1.4 %shard_map.74 = (f32[16,256]{1,0:T(8,128)S(1)}, f32[256,256]{1,0:T(8,128)S(1)}, f32[128,256]{1,0:T(8,128)S(1)}, f32[16,256]{1,0:T(8,128)S(1)}) custom-call(bf16[2048,256]{1,0:T(8,128)(2,1)S(1)} %get-tuple-element.52.turned_h, bf16[2048,256]{1,0:T(8,128)(2,1)S(1)} %get-tuple-element.53.turned_l, f32[256,256]{1,0:T(8,128)S(1)} %get-tuple-element.65.t_second, ...), custom_call_target="tpu_custom_call" | custom-call | flops 1073741824 | bytes 4194304 | tf_op jit(solution)/shard_map/pallas_call | solution.py:46
  25.8 7.8 %collective-permute-start.5 = (f32[256,256]{1,0:T(8,128)S(1)}, f32[256,256]{1,0:T(8,128)S(1)}, u32[]{:S(2)}, u32[]{:S(2)}) collective-permute-start(f32[256,256]{1,0:T(8,128)S(1)} %get-tuple-element.77), channel_id=1, source_target_pairs={{0,255},{1,0},{2,1},{3,2},{4,3},{5,4},{6,5},{7,6},{8,7},{9,8},{10,... | collective-permute-start | bytes 786440 | tf_op jit(solution)/shard_map/ppermute | solution.py:17
  33.6 7.8 %collective-permute-start.3 = (f32[128,256]{1,0:T(8,128)S(1)}, f32[128,256]{1,0:T(8,128)S(1)}, u32[]{:S(2)}, u32[]{:S(2)}) collective-permute-start(f32[128,256]{1,0:T(8,128)S(1)} %get-tuple-element.71), channel_id=1, source_target_pairs={{0,253},{1,254},{2,255},{3,0},{4,1},{5,2},{6,3},{7,4},{8,5},{9,6},... | collective-permute-start | bytes 393224 | tf_op jit(solution)/shard_map/ppermute | solution.py:17
  41.5 2.4 %shard_map.68 = (bf16[256,2048]{1,0:T(8,128)(2,1)S(1)}, bf16[256,2048]{1,0:T(8,128)(2,1)S(1)}, bf16[2048,256]{1,0:T(8,128)(2,1)S(1)}, bf16[2048,256]{1,0:T(8,128)(2,1)S(1)}) custom-call(f32[4,16,256,128]{3,2,1,0:T(8,128)} %target.7), custom_call_target="tpu_custom_call" | custom-call | flops 1073741824 | bytes 4194304 | tf_op jit(solution)/shard_map/pallas_call | solution.py:46
  43.9 1.7 %collective-permute-done.3.c = f32[128,256]{1,0:T(8,128)S(1)} collective-permute-done((f32[128,256]{1,0:T(8,128)S(1)}, f32[128,256]{1,0:T(8,128)S(1)}, u32[]{:S(2)}, u32[]{:S(2)}) %collective-permute-start.3) | collective-permute-done | bytes 131104 | tf_op jit(solution)/shard_map/ppermute | solution.py:17
  45.6 1.2 %shard_map.75 = (f32[256,256]{1,0:T(8,128)S(1)}, f32[256,256]{1,0:T(8,128)S(1)}, f32[256,256]{1,0:T(8,128)S(1)}, f32[128,256]{1,0:T(8,128)S(1)}) custom-call(f32[16,256]{1,0:T(8,128)S(1)} %get-tuple-element.70.a.refs_0_, f32[128,256]{1,0:T(8,128)S(1)} %collective-permute-done.3.c, f32[128,256]{1,0:T(8,128)S(1)} %collective-permute-done.4.refs_0_, ...), custom_call_target="tpu_custom_call" | custom-call | flops 1073741824 | bytes 4194304 | tf_op jit(solution)/shard_map/pallas_call | solution.py:46
  46.8 1.4 %shard_map.76 = (f32[16,256]{1,0:T(8,128)S(1)}, f32[256,256]{1,0:T(8,128)S(1)}, f32[128,256]{1,0:T(8,128)S(1)}, f32[16,256]{1,0:T(8,128)S(1)}) custom-call(bf16[2048,256]{1,0:T(8,128)(2,1)S(1)} %get-tuple-element.50.turned_h, bf16[2048,256]{1,0:T(8,128)(2,1)S(1)} %get-tuple-element.51.turned_l, f32[256,256]{1,0:T(8,128)S(1)} %get-tuple-element.74.t_second, ...), custom_call_target="tpu_custom_call" | custom-call | flops 1073741824 | bytes 4194304 | tf_op jit(solution)/shard_map/pallas_call | solution.py:46
  48.3 1.0 %collective-permute-start.9 = (f32[256,256]{1,0:T(8,128)S(1)}, f32[256,256]{1,0:T(8,128)S(1)}, u32[]{:S(2)}, u32[]{:S(2)}) collective-permute-start(f32[256,256]{1,0:T(8,128)S(1)} %get-tuple-element.87), channel_id=1, source_target_pairs={{0,255},{1,0},{2,1},{3,2},{4,3},{5,4},{6,5},{7,6},{8,7},{9,8},{10,... | collective-permute-start | bytes 786440 | tf_op jit(solution)/shard_map/ppermute | solution.py:17
  49.3 7.8 %collective-permute-start.7 = (f32[128,256]{1,0:T(8,128)S(1)}, f32[128,256]{1,0:T(8,128)S(1)}, u32[]{:S(2)}, u32[]{:S(2)}) collective-permute-start(f32[128,256]{1,0:T(8,128)S(1)} %get-tuple-element.81), channel_id=1, source_target_pairs={{0,253},{1,254},{2,255},{3,0},{4,1},{5,2},{6,3},{7,4},{8,5},{9,6},... | collective-permute-start | bytes 393224 | tf_op jit(solution)/shard_map/ppermute | solution.py:17
  57.1 2.4 %shard_map.67 = (bf16[256,2048]{1,0:T(8,128)(2,1)S(1)}, bf16[256,2048]{1,0:T(8,128)(2,1)S(1)}, bf16[2048,256]{1,0:T(8,128)(2,1)S(1)}, bf16[2048,256]{1,0:T(8,128)(2,1)S(1)}) custom-call(f32[4,16,256,128]{3,2,1,0:T(8,128)} %target.7), custom_call_target="tpu_custom_call" | custom-call | flops 1073741824 | bytes 4194304 | tf_op jit(solution)/shard_map/pallas_call | solution.py:46
  59.5 0.1 collective-permute-start.13
  59.6 0.8 %collective-permute-done.7.c = f32[128,256]{1,0:T(8,128)S(1)} collective-permute-done((f32[128,256]{1,0:T(8,128)S(1)}, f32[128,256]{1,0:T(8,128)S(1)}, u32[]{:S(2)}, u32[]{:S(2)}) %collective-permute-start.7) | collective-permute-done | bytes 131104 | tf_op jit(solution)/shard_map/ppermute | solution.py:17
  60.4 1.2 %shard_map.77 = (f32[256,256]{1,0:T(8,128)S(1)}, f32[256,256]{1,0:T(8,128)S(1)}, f32[256,256]{1,0:T(8,128)S(1)}, f32[128,256]{1,0:T(8,128)S(1)}) custom-call(f32[16,256]{1,0:T(8,128)S(1)} %get-tuple-element.80.a.refs_0_, f32[128,256]{1,0:T(8,128)S(1)} %collective-permute-done.7.c, f32[128,256]{1,0:T(8,128)S(1)} %collective-permute-done.8.refs_0_, ...), custom_call_target="tpu_custom_call" | custom-call | flops 1073741824 | bytes 4194304 | tf_op jit(solution)/shard_map/pallas_call | solution.py:46
  61.7 1.4 %shard_map.78 = (f32[16,256]{1,0:T(8,128)S(1)}, f32[256,256]{1,0:T(8,128)S(1)}, f32[128,256]{1,0:T(8,128)S(1)}) custom-call(bf16[2048,256]{1,0:T(8,128)(2,1)S(1)} %get-tuple-element.48.turned_h, bf16[2048,256]{1,0:T(8,128)(2,1)S(1)} %get-tuple-element.49.turned_l, f32[256,256]{1,0:T(8,128)S(1)} %get-tuple-element.84.t_second, ...), custom_call_target="tpu_custom_call" | custom-call | flops 1073741824 | bytes 4194304 | tf_op jit(solution)/shard_map/pallas_call | solution.py:46
  63.1 1.3 %collective-permute-start.12 = (f32[128,256]{1,0:T(8,128)S(1)}, f32[128,256]{1,0:T(8,128)S(1)}, u32[]{:S(2)}, u32[]{:S(2)}) collective-permute-start(f32[128,256]{1,0:T(8,128)S(1)} %get-tuple-element.92), channel_id=1, source_target_pairs={{0,9},{1,10},{2,11},{3,12},{4,13},{5,14},{6,15},{7,16},{8,17},{9,1... | collective-permute-start | bytes 393224 | tf_op jit(solution)/shard_map/ppermute | solution.py:17
  64.4 1.3 %collective-permute-start.10 = (f32[256,256]{1,0:T(8,128)S(1)}, f32[256,256]{1,0:T(8,128)S(1)}, u32[]{:S(2)}, u32[]{:S(2)}) collective-permute-start(f32[256,256]{1,0:T(8,128)S(1)} %get-tuple-element.91), channel_id=1, source_target_pairs={{0,3},{1,4},{2,5},{3,6},{4,7},{5,8},{6,9},{7,10},{8,11},{9,12},{10... | collective-permute-start | bytes 786440 | tf_op jit(solution)/shard_map/ppermute | solution.py:17
  65.7 0.6 copy.7
  66.3 4.1 %collective-permute-done.13 = f32[128,256]{1,0:T(8,128)S(1)} collective-permute-done((f32[128,256]{1,0:T(8,128)S(1)}, f32[128,256]{1,0:T(8,128)S(1)}, u32[]{:S(2)}, u32[]{:S(2)}) %collective-permute-start.13) | collective-permute-done | bytes 131104 | tf_op jit(solution)/shard_map/ppermute | solution.py:17
  70.4 0.5 collective-permute-done.12
  70.9 0.7 multiply_subtract_fusion.1
  71.6 12.1 %collective-permute-done.10 = f32[256,256]{1,0:T(8,128)S(1)} collective-permute-done((f32[256,256]{1,0:T(8,128)S(1)}, f32[256,256]{1,0:T(8,128)S(1)}, u32[]{:S(2)}, u32[]{:S(2)}) %collective-permute-start.10) | collective-permute-done | bytes 262176 | tf_op jit(solution)/shard_map/ppermute | solution.py:17
  83.6 0.7 multiply_subtract_fusion
  (17 shorter events, 0.0 us)
Async XLA Ops:
  0.6 2.5 %copy-start.2 = (f32[16,256]{1,0:T(8,128)S(1)}, f32[16,256]{1,0:T(8,128)}, u32[]{:S(2)}) copy-start(f32[16,256]{1,0:T(8,128)} %refs_0_.1) | copy-start | bytes 49156
  0.6 2.5 %copy-start = (f32[128,256]{1,0:T(8,128)S(1)}, f32[128,256]{1,0:T(8,128)}, u32[]{:S(2)}) copy-start(f32[128,256]{1,0:T(8,128)} %refs_2_.1) | copy-start | bytes 393220
  0.7 3.7 %copy-start.1 = (f32[256,256]{1,0:T(8,128)S(1)}, f32[256,256]{1,0:T(8,128)}, u32[]{:S(2)}) copy-start(f32[256,256]{1,0:T(8,128)} %refs_1_.1) | copy-start | bytes 786436
  5.7 18.6 %collective-permute-start.1 = (f32[256,256]{1,0:T(8,128)S(1)}, f32[256,256]{1,0:T(8,128)S(1)}, u32[]{:S(2)}, u32[]{:S(2)}) collective-permute-start(f32[256,256]{1,0:T(8,128)S(1)} %get-tuple-element.68), channel_id=1, source_target_pairs={{0,255},{1,0},{2,1},{3,2},{4,3},{5,4},{6,5},{7,6},{8,7},{9,8},{10,... | collective-permute-start | bytes 786440 | tf_op jit(solution)/shard_map/ppermute | solution.py:17
  9.0 15.4 %collective-permute-start.2 = (f32[256,256]{1,0:T(8,128)S(1)}, f32[256,256]{1,0:T(8,128)S(1)}, u32[]{:S(2)}, u32[]{:S(2)}) collective-permute-start(f32[256,256]{1,0:T(8,128)S(1)} %copy-done.1), channel_id=1, source_target_pairs={{0,255},{1,0},{2,1},{3,2},{4,3},{5,4},{6,5},{7,6},{8,7},{9,8},{10,... | collective-permute-start | bytes 786440 | tf_op jit(solution)/shard_map/ppermute | solution.py:17
  17.3 5.9 %collective-permute-start = (f32[128,256]{1,0:T(8,128)S(1)}, f32[128,256]{1,0:T(8,128)S(1)}, u32[]{:S(2)}, u32[]{:S(2)}) collective-permute-start(f32[128,256]{1,0:T(8,128)S(1)} %get-tuple-element.62), channel_id=1, source_target_pairs={{0,253},{1,254},{2,255},{3,0},{4,1},{5,2},{6,3},{7,4},{8,5},{9,6},... | collective-permute-start | bytes 393224 | tf_op jit(solution)/shard_map/ppermute | solution.py:17
  18.3 28.5 %collective-permute-start.6 = (f32[256,256]{1,0:T(8,128)S(1)}, f32[256,256]{1,0:T(8,128)S(1)}, u32[]{:S(2)}, u32[]{:S(2)}) collective-permute-start(f32[256,256]{1,0:T(8,128)S(1)} %get-tuple-element.68), channel_id=1, source_target_pairs={{0,254},{1,255},{2,0},{3,1},{4,2},{5,3},{6,4},{7,5},{8,6},{9,7},{1... | collective-permute-start | bytes 786440 | tf_op jit(solution)/shard_map/ppermute | solution.py:17
  25.8 21.0 %collective-permute-start.5 = (f32[256,256]{1,0:T(8,128)S(1)}, f32[256,256]{1,0:T(8,128)S(1)}, u32[]{:S(2)}, u32[]{:S(2)}) collective-permute-start(f32[256,256]{1,0:T(8,128)S(1)} %get-tuple-element.77), channel_id=1, source_target_pairs={{0,255},{1,0},{2,1},{3,2},{4,3},{5,4},{6,5},{7,6},{8,7},{9,8},{10,... | collective-permute-start | bytes 786440 | tf_op jit(solution)/shard_map/ppermute | solution.py:17
  33.6 10.2 %collective-permute-start.4 = (f32[128,256]{1,0:T(8,128)S(1)}, f32[128,256]{1,0:T(8,128)S(1)}, u32[]{:S(2)}, u32[]{:S(2)}) collective-permute-start(f32[128,256]{1,0:T(8,128)S(1)} %copy-done), channel_id=1, source_target_pairs={{0,250},{1,251},{2,252},{3,253},{4,254},{5,255},{6,0},{7,1},{8,2},... | collective-permute-start | bytes 393224 | tf_op jit(solution)/shard_map/ppermute | solution.py:17
  33.6 12.0 %collective-permute-start.3 = (f32[128,256]{1,0:T(8,128)S(1)}, f32[128,256]{1,0:T(8,128)S(1)}, u32[]{:S(2)}, u32[]{:S(2)}) collective-permute-start(f32[128,256]{1,0:T(8,128)S(1)} %get-tuple-element.71), channel_id=1, source_target_pairs={{0,253},{1,254},{2,255},{3,0},{4,1},{5,2},{6,3},{7,4},{8,5},{9,6},... | collective-permute-start | bytes 393224 | tf_op jit(solution)/shard_map/ppermute | solution.py:17
  48.3 13.4 %collective-permute-start.9 = (f32[256,256]{1,0:T(8,128)S(1)}, f32[256,256]{1,0:T(8,128)S(1)}, u32[]{:S(2)}, u32[]{:S(2)}) collective-permute-start(f32[256,256]{1,0:T(8,128)S(1)} %get-tuple-element.87), channel_id=1, source_target_pairs={{0,255},{1,0},{2,1},{3,2},{4,3},{5,4},{6,5},{7,6},{8,7},{9,8},{10,... | collective-permute-start | bytes 786440 | tf_op jit(solution)/shard_map/ppermute | solution.py:17
  49.3 10.3 %collective-permute-start.8 = (f32[128,256]{1,0:T(8,128)S(1)}, f32[128,256]{1,0:T(8,128)S(1)}, u32[]{:S(2)}, u32[]{:S(2)}) collective-permute-start(f32[128,256]{1,0:T(8,128)S(1)} %get-tuple-element.62), channel_id=1, source_target_pairs={{0,247},{1,248},{2,249},{3,250},{4,251},{5,252},{6,253},{7,254},{8... | collective-permute-start | bytes 393224 | tf_op jit(solution)/shard_map/ppermute | solution.py:17
  49.3 11.1 %collective-permute-start.7 = (f32[128,256]{1,0:T(8,128)S(1)}, f32[128,256]{1,0:T(8,128)S(1)}, u32[]{:S(2)}, u32[]{:S(2)}) collective-permute-start(f32[128,256]{1,0:T(8,128)S(1)} %get-tuple-element.81), channel_id=1, source_target_pairs={{0,253},{1,254},{2,255},{3,0},{4,1},{5,2},{6,3},{7,4},{8,5},{9,6},... | collective-permute-start | bytes 393224 | tf_op jit(solution)/shard_map/ppermute | solution.py:17
  59.5 10.9 %collective-permute-start.13 = (f32[128,256]{1,0:T(8,128)S(1)}, f32[128,256]{1,0:T(8,128)S(1)}, u32[]{:S(2)}, u32[]{:S(2)}) collective-permute-start(f32[128,256]{1,0:T(8,128)S(1)} %get-tuple-element.71), channel_id=1, source_target_pairs={{0,3},{1,4},{2,5},{3,6},{4,7},{5,8},{6,9},{7,10},{8,11},{9,12},{10... | collective-permute-start | bytes 393224 | tf_op jit(solution)/shard_map/ppermute | solution.py:17
  63.1 7.8 %collective-permute-start.12 = (f32[128,256]{1,0:T(8,128)S(1)}, f32[128,256]{1,0:T(8,128)S(1)}, u32[]{:S(2)}, u32[]{:S(2)}) collective-permute-start(f32[128,256]{1,0:T(8,128)S(1)} %get-tuple-element.92), channel_id=1, source_target_pairs={{0,9},{1,10},{2,11},{3,12},{4,13},{5,14},{6,15},{7,16},{8,17},{9,1... | collective-permute-start | bytes 393224 | tf_op jit(solution)/shard_map/ppermute | solution.py:17
  64.4 7.2 %collective-permute-start.11 = (f32[256,256]{1,0:T(8,128)S(1)}, f32[256,256]{1,0:T(8,128)S(1)}, u32[]{:S(2)}, u32[]{:S(2)}) collective-permute-start(f32[256,256]{1,0:T(8,128)S(1)} %get-tuple-element.77), channel_id=1, source_target_pairs={{0,1},{1,2},{2,3},{3,4},{4,5},{5,6},{6,7},{7,8},{8,9},{9,10},{10,1... | collective-permute-start | bytes 786440 | tf_op jit(solution)/shard_map/ppermute | solution.py:17
  64.4 19.2 %collective-permute-start.10 = (f32[256,256]{1,0:T(8,128)S(1)}, f32[256,256]{1,0:T(8,128)S(1)}, u32[]{:S(2)}, u32[]{:S(2)}) collective-permute-start(f32[256,256]{1,0:T(8,128)S(1)} %get-tuple-element.91), channel_id=1, source_target_pairs={{0,3},{1,4},{2,5},{3,6},{4,7},{5,8},{6,9},{7,10},{8,11},{9,12},{10... | collective-permute-start | bytes 786440 | tf_op jit(solution)/shard_map/ppermute | solution.py:17
where the time goes:
time: 84.5 us; the launch traced here: 84.4 us
  starting transfers between devices  39.9 us (47%)
  waiting for transfers between devices  21.6 us (26%)
  Pallas kernels  20.1 us (24%)
  other arithmetic  1.42 us (2%)
    ppermute x14, starting transfers between devices, sent(): lax.ppermute(array, 'blk', [(i, (i + by) % count) for i in range(count)])  39.9 us
    ppermute x14, waiting for transfers between devices, sent(): lax.ppermute(array, 'blk', [(i, (i + by) % count) for i in range(count)])  21.6 us
    pallas_call x12, Pallas kernels, kernel(): pl.pallas_call(body, out_shape=tuple(out_shape), in_specs=in_specs or vme...  20.1 us
  transfers between devices with their start and end apart: 14, of which 6 were waited for; matrix products, arithmetic and copies ran while one was open for 2% of the time, Pallas kernels for 16%

commit v1 on v0

--- a/solution.py
+++ b/solution.py
@@ -28,6 +28,13 @@
 
 def dot3(a, b):
     return dot(a[0], b[0]) + dot(a[0], b[1]) + dot(a[1], b[0])
+
+
+def turned_dot3(a, b):
+    def turned_dot(x, y):
+        return lax.dot_general(x, y, (((0,), (0,)), ((), ())), preferred_element_type=F32)
+
+    return turned_dot(a[0], b[0]) + turned_dot(a[0], b[1]) + turned_dot(a[1], b[0])
 
 
 def gram(x):
@@ -58,7 +65,7 @@
     _, first_rows, second_rows, third_rows = blocks.shape
     pairs = first_rows // 2
 
-    def body(target, natural_h, natural_l, turned_h, turned_l, buf, sem):
+    def body(target, high, low, buf, sem):
         def fetch(p):
             return pltpu.make_async_copy(target.at[s, pl.ds(2 * p, 2)], buf.at[p], sem.at[p])
 
@@ -67,16 +74,13 @@
         for p in range(pairs):
             fetch(p).wait()
             for h in range(2):
-                t = buf[p, h]
                 span = slice((2 * p + h) * third_rows, (2 * p + h + 1) * third_rows)
-                natural_h[:, span], natural_l[:, span] = split(t)
-                turned_h[span, :], turned_l[span, :] = split(t.T)
-
-    wide = first_rows * third_rows
-    natural, turned = like(second_rows, wide, dtype=BF16), like(wide, second_rows, dtype=BF16)
+                high[:, span], low[:, span] = split(buf[p, h])
+
+    shape = like(second_rows, first_rows * third_rows, dtype=BF16)
     return kernel(
         body,
-        (natural, natural, turned, turned),
+        (shape, shape),
         (pltpu.with_memory_space_constraint(blocks, pltpu.HBM),),
         in_specs=[pl.BlockSpec(memory_space=pltpu.HBM)],
         scratch_shapes=[
@@ -86,10 +90,10 @@
     )
 
 
-def second_side(first, third, older, natural_h, natural_l):
+def second_side(first, third, older, target):
     first_rows, rank = first.shape
     third_rows = third.shape[0]
-    second_rows, wide = natural_h.shape
+    second_rows, wide = target[0].shape
     chunks = 4
 
     def body(a, c, *refs):
@@ -119,37 +123,43 @@
     out = kernel(
         body,
         (like(second_rows, rank), like(rank, rank), like(rank, rank)) + ((like(third_rows, rank),) if olds else ()),
-        (first, third, *olds, natural_h, natural_l),
+        (first, third, *olds, *target),
         scratch_shapes=[pltpu.VMEM((wide, rank), BF16)] * 2,
     )
     return out if olds else (*out, third)
 
 
-def update(s, strata, rates, turned, target_second, grams, factors, vel_first, old_second):
+def step_second(s, rate, target_second, grams, second, older):
+    ahead = 1.0 if s == 0 else 1.0 + momentum
+
+    def body(t_second, gram_first, gram_third, b_ref, *refs):
+        b = b_ref[...]
+        gradient = dot3(split(b), split(gram_first[...] * gram_third[...])) - t_second[...]
+        base = ahead * b if older is None else ahead * b - momentum * refs[0][...]
+        refs[-1][...] = base - rate * gradient
+
+    olds = () if older is None else (older,)
+    (new,) = kernel(body, (like(*second.shape),), (target_second, *grams, second, *olds))
+    return new
+
+
+def step_others(s, strata, rates, target, grams, factors, vel_first):
     first_rows, rank = factors[0].shape
     third_rows = factors[2].shape[0]
     ahead = 1.0 if s == 0 else 1.0 + momentum
     last = s + 1 == strata
 
-    def body(turned_h, turned_l, t_second, gram_first, gram_third, *refs):
+    def body(target_h, target_l, gram_first, gram_third, *refs):
         a, b, c = (ref[...] for ref in refs[:3])
-        rest = list(refs[3:])
-        vel = momentum * rest.pop(0)[...] if s else None
-        old = rest.pop(0)[...] if old_second is not None else None
-        new_first, new_second, new_third = rest[:3]
-        contracted = rest[-1]
+        vel = momentum * refs[3][...] if s else None
+        new_first, new_third, *new_vel = refs[4:] if s else refs[3:]
         split_b = split(b)
-        contracted[...] = dot3((turned_h[...], turned_l[...]), split_b)
         gram_second = dot3(split(b.T), split_b)
-
-        g_second = dot3(split_b, split(gram_first[...] * gram_third[...])) - t_second[...]
-        base = ahead * b if old is None else ahead * b - momentum * old
-        new_second[...] = base - rates[1] * g_second
-
         g_third = jnp.zeros_like(c)
         rows = []
         for i in range(first_rows):
-            part = contracted[i * third_rows : (i + 1) * third_rows, :]
+            span = slice(i * third_rows, (i + 1) * third_rows)
+            part = turned_dot3((target_h[:, span], target_l[:, span]), split_b)
             rows.append(jnp.sum(part * c, axis=0, keepdims=True))
             g_third = g_third + part * refs[0][i : i + 1, :]
         g_third = dot3(split(c), split(gram_first[...] * gram_second)) - g_third
@@ -158,14 +168,11 @@
         step = rates[0] * g_first
         new_first[...] = a - step if vel is None else a + vel - step
         if not last:
-            rest[3][...] = -step if vel is None else vel - step
-
-    operands = (*turned, target_second, *grams, *factors)
-    operands += (vel_first,) if s else ()
-    operands += () if old_second is None else (old_second,)
-    shapes = [pltpu.VMEM(factors[0].shape, F32) if last else like(*factors[0].shape)]
-    shapes += [like(*x.shape) for x in factors[1:]] + ([] if last else [like(first_rows, rank)])
-    return kernel(body, shapes, operands, scratch_shapes=[pltpu.VMEM((first_rows * third_rows, rank), F32)])
+            new_vel[0][...] = -step if vel is None else vel - step
+
+    shapes = [pltpu.VMEM(factors[0].shape, F32) if last else like(*factors[0].shape), like(third_rows, rank)]
+    shapes += [] if last else [like(first_rows, rank)]
+    return kernel(body, shapes, (*target, *grams, *factors, *((vel_first,) if s else ())))
 
 
 def shards(blocks, first, second, third):
@@ -183,27 +190,22 @@
     old_second = old_third = None
     older = {}
     for s in range(strata):
-        natural_h, natural_l, *turned = prepare(s, blocks)
+        target = prepare(s, blocks)
         if s == 0:
             older["b1"] = sent(second, -1)
             older["c2"] = sent(third, -6)
+        came = second
         old_second, old_third = older.get(f"b{s}"), older.get(f"c{s}")
-        target_second, *grams, third = second_side(first, third, old_third, natural_h, natural_l)
-        first, second, third, *vel = update(
-            s,
-            strata,
-            rates,
-            turned,
-            target_second,
-            grams,
-            (first, second, third),
-            vel and vel[0],
-            old_second,
+        target_second, *grams, third = second_side(first, third, old_third, target)
+        new_second = step_second(s, rates[1], target_second, grams, second, old_second)
+        first, third, *vel = step_others(
+            s, strata, rates, target, grams, (first, second, third), vel and vel[0]
         )
+        second = new_second
         if s == 0:
-            older["b2"] = sent(second, -2)
             older["c3"] = sent(third, -9)
         if s == 1:
+            older["b2"] = sent(came, -1)
             back_second = sent(second, 1)
             back_third = sent(third, 3)
         if s + 1 < strata:

time: 84.5 us -> 81.1 us (0.960)
  starting transfers between devices: 39.9 us -> 36.9 us
  Pallas kernels: 20.1 us -> 17.8 us
  waiting for transfers between devices: 21.6 us -> 23.2 us
    ppermute x14, starting transfers between devices: 39.9 us -> 36.9 us  [sent(): lax.ppermute(array, 'blk', [(i, (i + by) % count) for i in range(count)])]
    pallas_call x12 -> x16, Pallas kernels: 20.1 us -> 17.8 us  [kernel(): pl.pallas_call(body, out_shape=tuple(out_shape), in_specs=in_specs or vme...]
    ppermute x14, waiting for transfers between devices: 21.6 us -> 23.2 us  [sent(): lax.ppermute(array, 'blk', [(i, (i + by) % count) for i in range(count)])]
  transfers between devices with their start and end apart: 14 -> 14, of which waited for: 6 -> 6; matrix products, arithmetic and copies ran while one was open for 2% -> 2% of each run, Pallas kernels for 16% -> 22%
where the time goes in v1:
time: 81.1 us; the launch traced here: 80.9 us
  starting transfers between devices  36.9 us (45%)
  waiting for transfers between devices  23.2 us (29%)
  Pallas kernels  17.8 us (22%)
  other arithmetic  1.42 us (2%)
  between operations  0.9 us (1%)
    ppermute x14, starting transfers between devices, sent(): lax.ppermute(array, 'blk', [(i, (i + by) % count) for i in range(count)])  36.9 us
    ppermute x14, waiting for transfers between devices, sent(): lax.ppermute(array, 'blk', [(i, (i + by) % count) for i in range(count)])  23.2 us
    pallas_call x16, Pallas kernels, kernel(): pl.pallas_call(body, out_shape=tuple(out_shape), in_specs=in_specs or vme...  17.8 us
  transfers between devices with their start and end apart: 14, of which 6 were waited for; matrix products, arithmetic and copies ran while one was open for 2% of the time, Pallas kernels for 22%

profile of v1, /device:TPU:1, one launch (start us, length us, event | category | flops | bytes accessed | tf_op | source)
XLA Modules:
  0.0 80.9 jit_solution(1740036518824808533)
XLA Ops:
  0.7 3.3 %collective-permute-start.4 = (f32[256,256]{1,0:T(8,128)}, f32[256,256]{1,0:T(8,128)S(1)}, u32[]{:S(2)}, u32[]{:S(2)}) collective-permute-start(f32[256,256]{1,0:T(8,128)} %b_ref.1), channel_id=1, source_target_pairs={{0,255},{1,0},{2,1},{3,2},{4,3},{5,4},{6,5},{7,6},{8,7},{9,8},{10,... | collective-permute-start | bytes 786440 | tf_op jit(solution)/shard_map/ppermute | solution.py:17
  3.9 1.6 %shard_map.70 = (bf16[256,2048]{1,0:T(8,128)(2,1)S(1)}, bf16[256,2048]{1,0:T(8,128)(2,1)S(1)}) custom-call(f32[4,16,256,128]{3,2,1,0:T(8,128)} %target.7), custom_call_target="tpu_custom_call" | custom-call | flops 1073741824 | bytes 4194304 | tf_op jit(solution)/shard_map/pallas_call | solution.py:53
  5.6 1.2 %shard_map.71 = (f32[256,256]{1,0:T(8,128)S(1)}, f32[256,256]{1,0:T(8,128)S(1)}, f32[256,256]{1,0:T(8,128)S(1)}) custom-call(f32[16,256]{1,0:T(8,128)S(1)} %copy-done.2, f32[128,256]{1,0:T(8,128)S(1)} %copy-done, bf16[256,2048]{1,0:T(8,128)(2,1)S(1)} %get-tuple-element.42.refs_0_.target_h, bf16[256,2048]{1,0:T(8,128)(2,1)S(1)} %get-tuple-element.43.refs_1_.target_l), custom_call_target="tpu_custom_call" | custom-call | flops 1073741824 | bytes 4194304 | tf_op jit(solution)/shard_map/pallas_call | solution.py:53
  6.8 0.3 shard_map.74
  7.1 8.3 %collective-permute-start.1 = (f32[256,256]{1,0:T(8,128)S(1)}, f32[256,256]{1,0:T(8,128)S(1)}, u32[]{:S(2)}, u32[]{:S(2)}) collective-permute-start(f32[256,256]{1,0:T(8,128)S(1)} %shard_map.74), channel_id=1, source_target_pairs={{0,255},{1,0},{2,1},{3,2},{4,3},{5,4},{6,5},{7,6},{8,7},{9,8},{10,... | collective-permute-start | bytes 786440 | tf_op jit(solution)/shard_map/ppermute | solution.py:17
  15.4 1.3 %shard_map.72 = (f32[16,256]{1,0:T(8,128)S(1)}, f32[128,256]{1,0:T(8,128)S(1)}, f32[16,256]{1,0:T(8,128)S(1)}) custom-call(bf16[256,2048]{1,0:T(8,128)(2,1)S(1)} %get-tuple-element.42.refs_0_.target_h, bf16[256,2048]{1,0:T(8,128)(2,1)S(1)} %get-tuple-element.43.refs_1_.target_l, f32[256,256]{1,0:T(8,128)S(1)} %get-tuple-element.44.gram_first, ...), custom_call_target="tpu_custom_call" | custom-call | flops 1073741824 | bytes 4194304 | tf_op jit(solution)/shard_map/pallas_call | solution.py:53
  16.8 1.1 %collective-permute-start = (f32[128,256]{1,0:T(8,128)S(1)}, f32[128,256]{1,0:T(8,128)S(1)}, u32[]{:S(2)}, u32[]{:S(2)}) collective-permute-start(f32[128,256]{1,0:T(8,128)S(1)} %get-tuple-element.47), channel_id=1, source_target_pairs={{0,253},{1,254},{2,255},{3,0},{4,1},{5,2},{6,3},{7,4},{8,5},{9,6},... | collective-permute-start | bytes 393224 | tf_op jit(solution)/shard_map/ppermute | solution.py:17
  17.9 1.3 %collective-permute-start.3 = (f32[128,256]{1,0:T(8,128)S(1)}, f32[128,256]{1,0:T(8,128)S(1)}, u32[]{:S(2)}, u32[]{:S(2)}) collective-permute-start(f32[128,256]{1,0:T(8,128)S(1)} %copy-done), channel_id=1, source_target_pairs={{0,250},{1,251},{2,252},{3,253},{4,254},{5,255},{6,0},{7,1},{8,2},... | collective-permute-start | bytes 393224 | tf_op jit(solution)/shard_map/ppermute | solution.py:17
  19.1 1.6 %shard_map.69 = (bf16[256,2048]{1,0:T(8,128)(2,1)S(1)}, bf16[256,2048]{1,0:T(8,128)(2,1)S(1)}) custom-call(f32[4,16,256,128]{3,2,1,0:T(8,128)} %target.7), custom_call_target="tpu_custom_call" | custom-call | flops 1073741824 | bytes 4194304 | tf_op jit(solution)/shard_map/pallas_call | solution.py:53
  20.8 2.1 %collective-permute-done.c.refs_2_ = f32[128,256]{1,0:T(8,128)S(1)} collective-permute-done((f32[128,256]{1,0:T(8,128)S(1)}, f32[128,256]{1,0:T(8,128)S(1)}, u32[]{:S(2)}, u32[]{:S(2)}) %collective-permute-start) | collective-permute-done | bytes 131104 | tf_op jit(solution)/shard_map/ppermute | solution.py:17
  22.8 1.2 %shard_map.73 = (f32[256,256]{1,0:T(8,128)S(1)}, f32[256,256]{1,0:T(8,128)S(1)}, f32[256,256]{1,0:T(8,128)S(1)}) custom-call(f32[16,256]{1,0:T(8,128)S(1)} %get-tuple-element.46.a.refs_0_, f32[128,256]{1,0:T(8,128)S(1)} %collective-permute-done.c.refs_2_, bf16[256,2048]{1,0:T(8,128)(2,1)S(1)} %get-tuple-element.40.refs_0_.target_h, ...), custom_call_target="tpu_custom_call" | custom-call | flops 1073741824 | bytes 4194304 | tf_op jit(solution)/shard_map/pallas_call | solution.py:53
  24.4 1.3 %collective-permute-start.5 = (f32[256,256]{1,0:T(8,128)S(1)}, f32[256,256]{1,0:T(8,128)S(1)}, u32[]{:S(2)}, u32[]{:S(2)}) collective-permute-start(f32[256,256]{1,0:T(8,128)S(1)} %shard_map.77), channel_id=1, source_target_pairs={{0,255},{1,0},{2,1},{3,2},{4,3},{5,4},{6,5},{7,6},{8,7},{9,8},{10,... | collective-permute-start | bytes 786440 | tf_op jit(solution)/shard_map/ppermute | solution.py:17
  25.7 6.0 %collective-permute-start.8 = (f32[256,256]{1,0:T(8,128)S(1)}, f32[256,256]{1,0:T(8,128)S(1)}, u32[]{:S(2)}, u32[]{:S(2)}) collective-permute-start(f32[256,256]{1,0:T(8,128)S(1)} %collective-permute-done.1.refs_1_.b_ref), channel_id=1, source_target_pairs={{0,255},{1,0},{2,1},{3,2},{4,3},{5,4},{6,5},{7,6},{8,7},{9,8},{10,... | collective-permute-start | bytes 786440 | tf_op jit(solution)/shard_map/ppermute | solution.py:17
  31.7 1.3 %shard_map.75 = (f32[16,256]{1,0:T(8,128)S(1)}, f32[128,256]{1,0:T(8,128)S(1)}, f32[16,256]{1,0:T(8,128)S(1)}) custom-call(bf16[256,2048]{1,0:T(8,128)(2,1)S(1)} %get-tuple-element.40.refs_0_.target_h, bf16[256,2048]{1,0:T(8,128)(2,1)S(1)} %get-tuple-element.41.refs_1_.target_l, f32[256,256]{1,0:T(8,128)S(1)} %get-tuple-element.48.gram_first, ...), custom_call_target="tpu_custom_call" | custom-call | flops 1073741824 | bytes 4194304 | tf_op jit(solution)/shard_map/pallas_call | solution.py:53
  33.0 1.9 %collective-permute-start.2 = (f32[128,256]{1,0:T(8,128)S(1)}, f32[128,256]{1,0:T(8,128)S(1)}, u32[]{:S(2)}, u32[]{:S(2)}) collective-permute-start(f32[128,256]{1,0:T(8,128)S(1)} %get-tuple-element.53), channel_id=1, source_target_pairs={{0,253},{1,254},{2,255},{3,0},{4,1},{5,2},{6,3},{7,4},{8,5},{9,6},... | collective-permute-start | bytes 393224 | tf_op jit(solution)/shard_map/ppermute | solution.py:17
  34.9 1.6 %shard_map.68 = (bf16[256,2048]{1,0:T(8,128)(2,1)S(1)}, bf16[256,2048]{1,0:T(8,128)(2,1)S(1)}) custom-call(f32[4,16,256,128]{3,2,1,0:T(8,128)} %target.7), custom_call_target="tpu_custom_call" | custom-call | flops 1073741824 | bytes 4194304 | tf_op jit(solution)/shard_map/pallas_call | solution.py:53
  36.6 2.4 %collective-permute-done.2.c = f32[128,256]{1,0:T(8,128)S(1)} collective-permute-done((f32[128,256]{1,0:T(8,128)S(1)}, f32[128,256]{1,0:T(8,128)S(1)}, u32[]{:S(2)}, u32[]{:S(2)}) %collective-permute-start.2) | collective-permute-done | bytes 131104 | tf_op jit(solution)/shard_map/ppermute | solution.py:17
  39.0 1.2 %shard_map.76 = (f32[256,256]{1,0:T(8,128)S(1)}, f32[256,256]{1,0:T(8,128)S(1)}, f32[256,256]{1,0:T(8,128)S(1)}, f32[128,256]{1,0:T(8,128)S(1)}) custom-call(f32[16,256]{1,0:T(8,128)S(1)} %get-tuple-element.52.a.refs_0_, f32[128,256]{1,0:T(8,128)S(1)} %collective-permute-done.2.c, f32[128,256]{1,0:T(8,128)S(1)} %collective-permute-done.3.refs_0_, ...), custom_call_target="tpu_custom_call" | custom-call | flops 1073741824 | bytes 4194304 | tf_op jit(solution)/shard_map/pallas_call | solution.py:53
  40.5 5.5 %collective-permute-start.9 = (f32[256,256]{1,0:T(8,128)S(1)}, f32[256,256]{1,0:T(8,128)S(1)}, u32[]{:S(2)}, u32[]{:S(2)}) collective-permute-start(f32[256,256]{1,0:T(8,128)S(1)} %shard_map.80), channel_id=1, source_target_pairs={{0,255},{1,0},{2,1},{3,2},{4,3},{5,4},{6,5},{7,6},{8,7},{9,8},{10,... | collective-permute-start | bytes 786440 | tf_op jit(solution)/shard_map/ppermute | solution.py:17
  46.0 1.3 %shard_map.78 = (f32[16,256]{1,0:T(8,128)S(1)}, f32[128,256]{1,0:T(8,128)S(1)}, f32[16,256]{1,0:T(8,128)S(1)}) custom-call(bf16[256,2048]{1,0:T(8,128)(2,1)S(1)} %get-tuple-element.38.refs_1_.target_h, bf16[256,2048]{1,0:T(8,128)(2,1)S(1)} %get-tuple-element.39.refs_2_.target_l, f32[256,256]{1,0:T(8,128)S(1)} %get-tuple-element.54.gram_first, ...), custom_call_target="tpu_custom_call" | custom-call | flops 1073741824 | bytes 4194304 | tf_op jit(solution)/shard_map/pallas_call | solution.py:53
  47.3 7.9 %collective-permute-start.6 = (f32[128,256]{1,0:T(8,128)S(1)}, f32[128,256]{1,0:T(8,128)S(1)}, u32[]{:S(2)}, u32[]{:S(2)}) collective-permute-start(f32[128,256]{1,0:T(8,128)S(1)} %get-tuple-element.60), channel_id=1, source_target_pairs={{0,253},{1,254},{2,255},{3,0},{4,1},{5,2},{6,3},{7,4},{8,5},{9,6},... | collective-permute-start | bytes 393224 | tf_op jit(solution)/shard_map/ppermute | solution.py:17
  55.2 1.6 %shard_map.67 = (bf16[256,2048]{1,0:T(8,128)(2,1)S(1)}, bf16[256,2048]{1,0:T(8,128)(2,1)S(1)}) custom-call(f32[4,16,256,128]{3,2,1,0:T(8,128)} %target.7), custom_call_target="tpu_custom_call" | custom-call | flops 1073741824 | bytes 4194304 | tf_op jit(solution)/shard_map/pallas_call | solution.py:53
  57.0 1.5 %collective-permute-done.6.c = f32[128,256]{1,0:T(8,128)S(1)} collective-permute-done((f32[128,256]{1,0:T(8,128)S(1)}, f32[128,256]{1,0:T(8,128)S(1)}, u32[]{:S(2)}, u32[]{:S(2)}) %collective-permute-start.6) | collective-permute-done | bytes 131104 | tf_op jit(solution)/shard_map/ppermute | solution.py:17
  58.5 1.2 %shard_map.79 = (f32[256,256]{1,0:T(8,128)S(1)}, f32[256,256]{1,0:T(8,128)S(1)}, f32[256,256]{1,0:T(8,128)S(1)}, f32[128,256]{1,0:T(8,128)S(1)}) custom-call(f32[16,256]{1,0:T(8,128)S(1)} %get-tuple-element.59.a.refs_0_, f32[128,256]{1,0:T(8,128)S(1)} %collective-permute-done.6.c, f32[128,256]{1,0:T(8,128)S(1)} %collective-permute-done.7.refs_0_, ...), custom_call_target="tpu_custom_call" | custom-call | flops 1073741824 | bytes 4194304 | tf_op jit(solution)/shard_map/pallas_call | solution.py:53
  59.8 1.3 %shard_map.81 = (f32[16,256]{1,0:T(8,128)S(1)}, f32[128,256]{1,0:T(8,128)S(1)}) custom-call(bf16[256,2048]{1,0:T(8,128)(2,1)S(1)} %get-tuple-element.36.refs_1_.target_h, bf16[256,2048]{1,0:T(8,128)(2,1)S(1)} %get-tuple-element.37.refs_2_.target_l, f32[256,256]{1,0:T(8,128)S(1)} %get-tuple-element.61.gram_first, ...), custom_call_target="tpu_custom_call" | custom-call | flops 1073741824 | bytes 4194304 | tf_op jit(solution)/shard_map/pallas_call | solution.py:53
  61.3 0.3 shard_map.82
  61.7 0.6 copy.7
  62.3 5.4 %collective-permute-done.13 = f32[128,256]{1,0:T(8,128)S(1)} collective-permute-done((f32[128,256]{1,0:T(8,128)S(1)}, f32[128,256]{1,0:T(8,128)S(1)}, u32[]{:S(2)}, u32[]{:S(2)}) %collective-permute-start.13) | collective-permute-done | bytes 131104 | tf_op jit(solution)/shard_map/ppermute | solution.py:17
  67.6 1.2 %collective-permute-done.12 = f32[128,256]{1,0:T(8,128)S(1)} collective-permute-done((f32[128,256]{1,0:T(8,128)S(1)}, f32[128,256]{1,0:T(8,128)S(1)}, u32[]{:S(2)}, u32[]{:S(2)}) %collective-permute-start.12) | collective-permute-done | bytes 131104 | tf_op jit(solution)/shard_map/ppermute | solution.py:17
  68.9 0.7 multiply_subtract_fusion.1
  69.6 10.6 %collective-permute-done.10 = f32[256,256]{1,0:T(8,128)S(1)} collective-permute-done((f32[256,256]{1,0:T(8,128)S(1)}, f32[256,256]{1,0:T(8,128)S(1)}, u32[]{:S(2)}, u32[]{:S(2)}) %collective-permute-start.10) | collective-permute-done | bytes 262176 | tf_op jit(solution)/shard_map/ppermute | solution.py:17
  80.2 0.7 multiply_subtract_fusion
  (21 shorter events, 0.9 us)
Async XLA Ops:
  0.6 6.2 %copy-start.1 = (f32[256,256]{1,0:T(8,128)S(1)}, f32[256,256]{1,0:T(8,128)}, u32[]{:S(2)}) copy-start(f32[256,256]{1,0:T(8,128)} %b_ref.1) | copy-start | bytes 786436
  0.6 4.9 %copy-start.2 = (f32[16,256]{1,0:T(8,128)S(1)}, f32[16,256]{1,0:T(8,128)}, u32[]{:S(2)}) copy-start(f32[16,256]{1,0:T(8,128)} %refs_0_.1) | copy-start | bytes 49156
  0.7 4.9 %copy-start = (f32[128,256]{1,0:T(8,128)S(1)}, f32[128,256]{1,0:T(8,128)}, u32[]{:S(2)}) copy-start(f32[128,256]{1,0:T(8,128)} %refs_2_.1) | copy-start | bytes 393220
  0.7 23.4 %collective-permute-start.4 = (f32[256,256]{1,0:T(8,128)}, f32[256,256]{1,0:T(8,128)S(1)}, u32[]{:S(2)}, u32[]{:S(2)}) collective-permute-start(f32[256,256]{1,0:T(8,128)} %b_ref.1), channel_id=1, source_target_pairs={{0,255},{1,0},{2,1},{3,2},{4,3},{5,4},{6,5},{7,6},{8,7},{9,8},{10,... | collective-permute-start | bytes 786440 | tf_op jit(solution)/shard_map/ppermute | solution.py:17
  7.1 16.9 %collective-permute-start.1 = (f32[256,256]{1,0:T(8,128)S(1)}, f32[256,256]{1,0:T(8,128)S(1)}, u32[]{:S(2)}, u32[]{:S(2)}) collective-permute-start(f32[256,256]{1,0:T(8,128)S(1)} %shard_map.74), channel_id=1, source_target_pairs={{0,255},{1,0},{2,1},{3,2},{4,3},{5,4},{6,5},{7,6},{8,7},{9,8},{10,... | collective-permute-start | bytes 786440 | tf_op jit(solution)/shard_map/ppermute | solution.py:17
  16.8 6.1 %collective-permute-start = (f32[128,256]{1,0:T(8,128)S(1)}, f32[128,256]{1,0:T(8,128)S(1)}, u32[]{:S(2)}, u32[]{:S(2)}) collective-permute-start(f32[128,256]{1,0:T(8,128)S(1)} %get-tuple-element.47), channel_id=1, source_target_pairs={{0,253},{1,254},{2,255},{3,0},{4,1},{5,2},{6,3},{7,4},{8,5},{9,6},... | collective-permute-start | bytes 393224 | tf_op jit(solution)/shard_map/ppermute | solution.py:17
  17.9 18.7 %collective-permute-start.3 = (f32[128,256]{1,0:T(8,128)S(1)}, f32[128,256]{1,0:T(8,128)S(1)}, u32[]{:S(2)}, u32[]{:S(2)}) collective-permute-start(f32[128,256]{1,0:T(8,128)S(1)} %copy-done), channel_id=1, source_target_pairs={{0,250},{1,251},{2,252},{3,253},{4,254},{5,255},{6,0},{7,1},{8,2},... | collective-permute-start | bytes 393224 | tf_op jit(solution)/shard_map/ppermute | solution.py:17
  24.4 15.9 %collective-permute-start.5 = (f32[256,256]{1,0:T(8,128)S(1)}, f32[256,256]{1,0:T(8,128)S(1)}, u32[]{:S(2)}, u32[]{:S(2)}) collective-permute-start(f32[256,256]{1,0:T(8,128)S(1)} %shard_map.77), channel_id=1, source_target_pairs={{0,255},{1,0},{2,1},{3,2},{4,3},{5,4},{6,5},{7,6},{8,7},{9,8},{10,... | collective-permute-start | bytes 786440 | tf_op jit(solution)/shard_map/ppermute | solution.py:17
  25.7 14.6 %collective-permute-start.8 = (f32[256,256]{1,0:T(8,128)S(1)}, f32[256,256]{1,0:T(8,128)S(1)}, u32[]{:S(2)}, u32[]{:S(2)}) collective-permute-start(f32[256,256]{1,0:T(8,128)S(1)} %collective-permute-done.1.refs_1_.b_ref), channel_id=1, source_target_pairs={{0,255},{1,0},{2,1},{3,2},{4,3},{5,4},{6,5},{7,6},{8,7},{9,8},{10,... | collective-permute-start | bytes 786440 | tf_op jit(solution)/shard_map/ppermute | solution.py:17
  33.0 6.0 %collective-permute-start.2 = (f32[128,256]{1,0:T(8,128)S(1)}, f32[128,256]{1,0:T(8,128)S(1)}, u32[]{:S(2)}, u32[]{:S(2)}) collective-permute-start(f32[128,256]{1,0:T(8,128)S(1)} %get-tuple-element.53), channel_id=1, source_target_pairs={{0,253},{1,254},{2,255},{3,0},{4,1},{5,2},{6,3},{7,4},{8,5},{9,6},... | collective-permute-start | bytes 393224 | tf_op jit(solution)/shard_map/ppermute | solution.py:17
  34.9 22.0 %collective-permute-start.7 = (f32[128,256]{1,0:T(8,128)S(1)}, f32[128,256]{1,0:T(8,128)S(1)}, u32[]{:S(2)}, u32[]{:S(2)}) collective-permute-start(f32[128,256]{1,0:T(8,128)S(1)} %get-tuple-element.47), channel_id=1, source_target_pairs={{0,247},{1,248},{2,249},{3,250},{4,251},{5,252},{6,253},{7,254},{8... | collective-permute-start | bytes 393224 | tf_op jit(solution)/shard_map/ppermute | solution.py:17
  40.5 19.2 %collective-permute-start.9 = (f32[256,256]{1,0:T(8,128)S(1)}, f32[256,256]{1,0:T(8,128)S(1)}, u32[]{:S(2)}, u32[]{:S(2)}) collective-permute-start(f32[256,256]{1,0:T(8,128)S(1)} %shard_map.80), channel_id=1, source_target_pairs={{0,255},{1,0},{2,1},{3,2},{4,3},{5,4},{6,5},{7,6},{8,7},{9,8},{10,... | collective-permute-start | bytes 786440 | tf_op jit(solution)/shard_map/ppermute | solution.py:17
  47.3 11.2 %collective-permute-start.6 = (f32[128,256]{1,0:T(8,128)S(1)}, f32[128,256]{1,0:T(8,128)S(1)}, u32[]{:S(2)}, u32[]{:S(2)}) collective-permute-start(f32[128,256]{1,0:T(8,128)S(1)} %get-tuple-element.60), channel_id=1, source_target_pairs={{0,253},{1,254},{2,255},{3,0},{4,1},{5,2},{6,3},{7,4},{8,5},{9,6},... | collective-permute-start | bytes 393224 | tf_op jit(solution)/shard_map/ppermute | solution.py:17
  56.9 10.8 %collective-permute-start.13 = (f32[128,256]{1,0:T(8,128)S(1)}, f32[128,256]{1,0:T(8,128)S(1)}, u32[]{:S(2)}, u32[]{:S(2)}) collective-permute-start(f32[128,256]{1,0:T(8,128)S(1)} %get-tuple-element.53), channel_id=1, source_target_pairs={{0,3},{1,4},{2,5},{3,6},{4,7},{5,8},{6,9},{7,10},{8,11},{9,12},{10... | collective-permute-start | bytes 393224 | tf_op jit(solution)/shard_map/ppermute | solution.py:17
  61.1 7.8 %collective-permute-start.12 = (f32[128,256]{1,0:T(8,128)S(1)}, f32[128,256]{1,0:T(8,128)S(1)}, u32[]{:S(2)}, u32[]{:S(2)}) collective-permute-start(f32[128,256]{1,0:T(8,128)S(1)} %get-tuple-element.68), channel_id=1, source_target_pairs={{0,9},{1,10},{2,11},{3,12},{4,13},{5,14},{6,15},{7,16},{8,17},{9,1... | collective-permute-start | bytes 393224 | tf_op jit(solution)/shard_map/ppermute | solution.py:17
  61.2 8.4 %collective-permute-start.11 = (f32[256,256]{1,0:T(8,128)S(1)}, f32[256,256]{1,0:T(8,128)S(1)}, u32[]{:S(2)}, u32[]{:S(2)}) collective-permute-start(f32[256,256]{1,0:T(8,128)S(1)} %shard_map.77), channel_id=1, source_target_pairs={{0,1},{1,2},{2,3},{3,4},{4,5},{5,6},{6,7},{7,8},{8,9},{9,10},{10,1... | collective-permute-start | bytes 786440 | tf_op jit(solution)/shard_map/ppermute | solution.py:17
  61.6 18.6 %collective-permute-start.10 = (f32[256,256]{1,0:T(8,128)S(1)}, f32[256,256]{1,0:T(8,128)S(1)}, u32[]{:S(2)}, u32[]{:S(2)}) collective-permute-start(f32[256,256]{1,0:T(8,128)S(1)} %shard_map.82), channel_id=1, source_target_pairs={{0,3},{1,4},{2,5},{3,6},{4,7},{5,8},{6,9},{7,10},{8,11},{9,12},{10... | collective-permute-start | bytes 786440 | tf_op jit(solution)/shard_map/ppermute | solution.py:17
